TPU v7x, 32 devices: a whole 2x2x4 slice. The times are simulated.
32 devices in a mesh: blk: 8 (over z, y), rep: 4 (over x, core).
Axes of the slice: x: 2, y: 2, z: 4, core: 2. Of those that a mesh axis runs over, the one named last changes fastest.
Arguments:
- features: bfloat16 [8192, 256], P(('blk', 'rep')), may hold values from -6 to 6
- tiles: bfloat16 [8, 64, 128, 128], P('blk', 'rep'), may hold values from -0.25 to 0.25
- tile_rows: int32 [8, 64], P('blk', 'rep'), may hold values from 0 to 7
- tile_cols: int32 [8, 64], P('blk', 'rep'), may hold values from 0 to 15
- counts: int32 [8, 4], P('blk', 'rep'), may hold values from 4 to 16
- weight: bfloat16 [256, 256], replicated, may hold values from -0.375 to 0.375
- bias: float32 [256], replicated, may hold values from -3 to 3
- cotangent: bfloat16 [8192, 256], P(('blk', 'rep')), may hold values from -6 to 6
Outputs:
- activations: bfloat16 [8192, 256], P(('blk', 'rep'))
- feature_grad: bfloat16 [8192, 256], P(('blk', 'rep'))
- weight_grad: float32 [256, 256], replicated
- bias_grad: float32 [256], replicated
All inputs are finite; a program needn't handle non-finite values.
Results may differ from a plain program's by a relative error of at most 0.006.
Values may be sent and summed in bfloat16 or wider, within the bound.
A program may use at most 64 MiB of HBM per device.

v0:
```python
import jax
import jax.numpy as jnp
from jax import lax
from jax.sharding import PartitionSpec as P


def shifted(block, axis, distance):
    devices = range(lax.axis_size(axis))
    route = [((i - distance) % len(devices), i) for i in devices]
    return lax.ppermute(block, axis, route)


def per_device(features, tiles, tile_rows, tile_cols, counts, weight, bias, cotangent):
    highest = lax.Precision.HIGHEST
    tile_size = tiles.shape[2]
    slot_count = tiles.shape[1]
    feat_width = features.shape[1]
    own_rows = features.shape[0]
    own_tiles = own_rows // tile_size
    rep_count = lax.axis_size("rep")
    blk_count = lax.axis_size("blk")
    slot_tiles = tiles[0]
    row_index = tile_rows[0]
    col_index = tile_cols[0]
    slot_live = (jnp.arange(slot_count, dtype=jnp.int32) < counts[0, 0]).astype(jnp.float32)
    wanted = col_index[:, None] * tile_size + jnp.arange(tile_size, dtype=jnp.int32)[None, :]
    piece = lax.all_gather(features, "blk", axis=0, tiled=True)
    piece_count = piece.shape[0]
    inside = (wanted >= 0) & (wanted < piece_count)
    clipped = jnp.clip(wanted, 0, piece_count - 1)
    taken = jnp.take(piece, clipped.reshape(-1), axis=0).reshape(slot_count, tile_size, feat_width)
    selected = jnp.where(inside[:, :, None], taken, jnp.zeros((), jnp.bfloat16))
    partial_value = jnp.einsum(
        "sij,sjf->sif", slot_tiles, selected, preferred_element_type=jnp.float32
    )
    row_onehot = (
        row_index[:, None] == jnp.arange(rep_count * own_tiles, dtype=jnp.int32)[None, :]
    ).astype(jnp.float32) * slot_live[:, None]
    summed = jnp.einsum("st,sif->tif", row_onehot, partial_value, precision=highest)
    aggregate = lax.psum_scatter(
        summed.reshape(rep_count * own_rows, feat_width), "rep", scatter_dimension=0, tiled=True
    ).astype(jnp.bfloat16)
    pre_act = jnp.dot(aggregate, weight, preferred_element_type=jnp.float32) + bias[None, :]
    logistic = jax.nn.sigmoid(pre_act)
    activations = (pre_act * logistic).astype(jnp.bfloat16)
    act_grad = (
        cotangent.astype(jnp.float32) * logistic * (1.0 + pre_act * (1.0 - logistic))
    ).astype(jnp.bfloat16)
    local_weight = jnp.dot(aggregate.T, act_grad, preferred_element_type=jnp.float32)
    local_bias = jnp.sum(act_grad.astype(jnp.float32), axis=0)
    weight_grad, bias_grad = lax.psum((local_weight, local_bias), ("blk", "rep"))
    scale_factor = 1.0 / (blk_count * rep_count)
    weight_grad = weight_grad * scale_factor
    bias_grad = bias_grad * scale_factor
    agg_grad = jnp.dot(act_grad, weight.T, preferred_element_type=jnp.float32).astype(jnp.bfloat16)
    gathered = lax.all_gather(agg_grad, "rep", axis=0, tiled=True).reshape(
        rep_count * own_tiles, tile_size, feat_width
    )
    chosen = jnp.take(gathered, row_index, axis=0)
    contribution = (
        jnp.einsum("sij,sif->sjf", slot_tiles, chosen, preferred_element_type=jnp.float32)
        * slot_live[:, None, None]
    )

    def column_terms(first_row, row_count):
        targets = first_row // tile_size + jnp.arange(row_count // tile_size, dtype=jnp.int32)
        col_onehot = (col_index[:, None] == targets[None, :]).astype(jnp.float32)
        placed = jnp.einsum("sp,sjf->pjf", col_onehot, contribution, precision=highest)
        return placed.reshape(row_count, feat_width)

    own_block = lax.axis_index("blk")

    def travel_step(step_index, travelling):
        source_block = (own_block - step_index) % blk_count
        travelling = travelling + column_terms(source_block * own_rows, own_rows)
        return shifted(travelling, "blk", 1)

    feature_sum = lax.fori_loop(
        0, blk_count, travel_step, jnp.zeros((own_rows, feat_width), jnp.float32)
    )
    feature_grad = feature_sum.astype(jnp.bfloat16)
    return (activations, feature_grad, weight_grad, bias_grad)


def solution(mesh):
    in_specs = (
        P(("blk", "rep"), None),
        P("blk", "rep", None, None),
        P("blk", "rep"),
        P("blk", "rep"),
        P("blk", "rep"),
        P(),
        P(),
        P(("blk", "rep"), None),
    )
    out_specs = (P(("blk", "rep"), None), P(("blk", "rep"), None), P(), P())
    return jax.shard_map(
        per_device, mesh=mesh, in_specs=in_specs, out_specs=out_specs, check_vma=False
    )
```

profile of v0, /device:TPU:10, one launch (start us, length us, event | category | flops | bytes accessed | tf_op | source)
XLA Modules:
  0.0 242.8 jit_solution(17766153802447288838)
XLA Ops:
  7.2 0.7 all-gather.2.cloned.1.call-update
  8.6 0.7 multiply_bitcast_fusion.1
  9.3 0.1 fusion.25
  9.4 0.1 fusion.22
  9.5 40.9 %all-gather.2.cloned.1.call-done = bf16[2048,256]{1,0:T(8,128)(2,1)} async-done(((bf16[256,256]{1,0:T(8,128)(2,1)}), bf16[2048,256]{1,0:T(8,128)(2,1)}) %all-gather.2.cloned.1.call-update) | async-done | bytes 1048592 | tf_op jit(solution)/shard_map/all_gather | solution.py:27
  50.4 9.8 %gather_fusion = bf16[2048,256]{1,0:T(8,128)(2,1)} fusion(bf16[2048,256]{1,0:T(8,128)(2,1)} %all-gather.2.cloned.1.call-done, s32[2048]{0:T(1024)S(1)} %broadcast_clamp_fusion), kind=kCustom, calls=%fused_computation | custom fusion | bytes 2105344 | tf_op jit(solution)/shard_map/jit(_take)/gather | solution.py:31
  60.2 2.3 fusion.8
  62.6 2.1 copy.18
  64.7 2.7 %fusion.5 = f32[8,128,256]{2,0,1:T(8,128)S(1)} fusion(f32[16,256,128]{1,0,2:T(8,128)} %copy.18, f32[16]{0:T(128)S(1)} %compare_convert_fusion, s32[16]{0:T(128)S(1)} %bitcast.53), kind=kOutput, calls=%fused_computation.9 | convolution fusion | flops 50331904 | bytes 3145856 | tf_op jit(solution)/shard_map/st,sif->tif/dot_general | solution.py:39
  67.4 1.3 copy.15
  68.7 0.0 all-reduce.2.cloned.1.call-start
  68.8 23.8 %reduce-scatter.2.cloned.1.call-done = f32[256,256]{1,0:T(8,128)} async-done(((f32[1024,256]{1,0:T(8,128)}), f32[256,256]{1,0:T(8,128)}) %reduce-scatter.2.cloned.1.call-update) | async-done | bytes 262160 | tf_op jit(solution)/shard_map/reduce_scatter | solution.py:40
  92.7 2.0 convert_reduce_fusion
  94.6 0.2 convolution_convert_fusion
  94.9 0.9 fusion.19
  95.8 7.2 %all_gather.7 = bf16[1024,256]{1,0:T(8,128)(2,1)S(1)} all-gather(bf16[256,256]{1,0:T(8,128)(2,1)S(1)} %convolution_convert_fusion), channel_id=1, replica_groups=mesh['blk'=8,'rep'=4] {'rep'}, dimensions={0}, use_global_device_ids=true | all-gather | bytes 655360 | tf_op jit(solution)/shard_map/all_gather | solution.py:56
  103.0 0.6 gather_fusion.1
  103.6 1.9 multiply_bitcast_fusion
  105.5 2.3 copy.17
  107.8 78.2 %while.15 = (s32[]{:T(128)}, f32[256,256]{1,0:T(8,128)S(1)}, s32[1,16]{1,0:T(1,128)S(1)}, s32[]{:T(128)}, f32[16,128,256]{2,0,1:T(8,128)S(1)}, /*index=5*/s32[]{...) while((s32[]{:T(128)}, f32[256,256]{1,0:T(8,128)S(1)}, ...), condition=%wide.region_2.3_spmd, body=%wide.region_1.2_spmd.sunk | while | flops 12648512 | bytes 4719116 | solution.py:78
  107.9 0.8 fusion.46
  108.8 1.5 collective-permute-start
  110.3 8.3 %collective-permute-done = f32[256,256]{1,0:T(8,128)S(1)} collective-permute-done((f32[256,256]{1,0:T(8,128)S(1)}, f32[256,256]{1,0:T(8,128)S(1)}, u32[]{:S(2)}, u32[]{:S(2)}) %collective-permute-start) | collective-permute-done | bytes 262176 | tf_op jit(solution)/shard_map/while/body/eval_jaxpr/ppermute | solution.py:10
  118.6 0.8 fusion.46
  119.5 0.5 collective-permute-start
  120.0 8.6 %collective-permute-done = f32[256,256]{1,0:T(8,128)S(1)} collective-permute-done((f32[256,256]{1,0:T(8,128)S(1)}, f32[256,256]{1,0:T(8,128)S(1)}, u32[]{:S(2)}, u32[]{:S(2)}) %collective-permute-start) | collective-permute-done | bytes 262176 | tf_op jit(solution)/shard_map/while/body/eval_jaxpr/ppermute | solution.py:10
  128.5 0.8 fusion.46
  129.4 0.1 collective-permute-start
  129.5 7.8 %collective-permute-done = f32[256,256]{1,0:T(8,128)S(1)} collective-permute-done((f32[256,256]{1,0:T(8,128)S(1)}, f32[256,256]{1,0:T(8,128)S(1)}, u32[]{:S(2)}, u32[]{:S(2)}) %collective-permute-start) | collective-permute-done | bytes 262176 | tf_op jit(solution)/shard_map/while/body/eval_jaxpr/ppermute | solution.py:10
  137.3 0.8 fusion.46
  138.2 0.1 collective-permute-start
  138.3 7.8 %collective-permute-done = f32[256,256]{1,0:T(8,128)S(1)} collective-permute-done((f32[256,256]{1,0:T(8,128)S(1)}, f32[256,256]{1,0:T(8,128)S(1)}, u32[]{:S(2)}, u32[]{:S(2)}) %collective-permute-start) | collective-permute-done | bytes 262176 | tf_op jit(solution)/shard_map/while/body/eval_jaxpr/ppermute | solution.py:10
  146.1 0.8 fusion.46
  147.0 0.1 collective-permute-start
  147.1 8.3 %collective-permute-done = f32[256,256]{1,0:T(8,128)S(1)} collective-permute-done((f32[256,256]{1,0:T(8,128)S(1)}, f32[256,256]{1,0:T(8,128)S(1)}, u32[]{:S(2)}, u32[]{:S(2)}) %collective-permute-start) | collective-permute-done | bytes 262176 | tf_op jit(solution)/shard_map/while/body/eval_jaxpr/ppermute | solution.py:10
  155.4 0.8 fusion.46
  156.3 0.1 collective-permute-start
  156.4 9.1 %collective-permute-done = f32[256,256]{1,0:T(8,128)S(1)} collective-permute-done((f32[256,256]{1,0:T(8,128)S(1)}, f32[256,256]{1,0:T(8,128)S(1)}, u32[]{:S(2)}, u32[]{:S(2)}) %collective-permute-start) | collective-permute-done | bytes 262176 | tf_op jit(solution)/shard_map/while/body/eval_jaxpr/ppermute | solution.py:10
  165.5 0.8 fusion.46
  166.4 0.1 collective-permute-start
  166.5 9.4 %collective-permute-done = f32[256,256]{1,0:T(8,128)S(1)} collective-permute-done((f32[256,256]{1,0:T(8,128)S(1)}, f32[256,256]{1,0:T(8,128)S(1)}, u32[]{:S(2)}, u32[]{:S(2)}) %collective-permute-start) | collective-permute-done | bytes 262176 | tf_op jit(solution)/shard_map/while/body/eval_jaxpr/ppermute | solution.py:10
  175.9 0.8 fusion.46
  176.8 0.1 collective-permute-start
  176.8 9.1 %collective-permute-done = f32[256,256]{1,0:T(8,128)S(1)} collective-permute-done((f32[256,256]{1,0:T(8,128)S(1)}, f32[256,256]{1,0:T(8,128)S(1)}, u32[]{:S(2)}, u32[]{:S(2)}) %collective-permute-start) | collective-permute-done | bytes 262176 | tf_op jit(solution)/shard_map/while/body/eval_jaxpr/ppermute | solution.py:10
  186.0 0.7 convert_element_type.42
  186.7 47.3 %psum.15 = f32[256]{0:T(256)S(1)} all-reduce(f32[256]{0:T(256)S(1)} %get-tuple-element.160), channel_id=1, replica_groups=mesh['blk'=8,'rep'=4] {'blk','rep'}, use_global_device_ids=true, to_apply=%region_5.6 | all-reduce | flops 256 | bytes 2048 | tf_op jit(solution)/shard_map/psum | solution.py:51
  234.0 0.6 broadcast_multiply_fusion.1
  234.6 1.7 broadcast_multiply_fusion
  (50 shorter events, 0.7 us)
Async XLA Ops:
  7.2 53.1 %copy-start = (bf16[1,16,128,128]{3,2,1,0:T(8,128)(2,1)S(1)}, bf16[1,16,128,128]{3,2,1,0:T(8,128)(2,1)}, u32[]{:S(2)}) copy-start(bf16[1,16,128,128]{3,2,1,0:T(8,128)(2,1)} %param.11) | copy-start | bytes 1572868
  7.2 43.2 %all-gather.2.cloned.1.call-start = ((), (), s32[]{:S(2)}) async-start(), calls=%async_computation.1 | async-start | bytes 1179648 | tf_op jit(solution)/shard_map/all_gather | solution.py:27
  7.9 84.7 %reduce-scatter.2.cloned.1.call-start = ((), (), s32[]{:S(2)}) async-start(), calls=%async_computation.2 | async-start | bytes 1310720 | tf_op jit(solution)/shard_map/reduce_scatter | solution.py:40
  62.6 2.1 copy-start.4
  67.4 25.3 %copy-start.2 = (bf16[256,256]{1,0:T(8,128)(2,1)S(1)}, bf16[256,256]{1,0:T(8,128)(2,1)}, u32[]{:S(2)}) copy-start(bf16[256,256]{1,0:T(8,128)(2,1)} %param.15) | copy-start | bytes 393220
  67.4 25.3 %copy-start.5 = (bf16[256,256]{1,0:T(8,128)(2,1)S(1)}, bf16[256,256]{1,0:T(8,128)(2,1)}, u32[]{:S(2)}) copy-start(bf16[256,256]{1,0:T(8,128)(2,1)} %param.17) | copy-start | bytes 393220
  67.4 25.2 %copy-start.6 = (f32[256]{0:T(256)S(1)}, f32[256]{0:T(256)}, u32[]{:S(2)}) copy-start(f32[256]{0:T(256)} %param.16) | copy-start | bytes 3076
  68.7 165.8 %all-reduce.2.cloned.1.call-start = ((), (), s32[]{:S(2)}) async-start(), calls=%async_computation.3 | async-start | bytes 524288 | tf_op jit(solution)/shard_map/psum | solution.py:51
  92.6 2.2 copy-start.1
  105.5 2.3 copy-start.3
  108.8 9.8 %collective-permute-start = (f32[256,256]{1,0:T(8,128)S(1)}, f32[256,256]{1,0:T(8,128)S(1)}, u32[]{:S(2)}, u32[]{:S(2)}) collective-permute-start(f32[256,256]{1,0:T(8,128)S(1)} %bitcast_add_fusion.2), channel_id=1, source_target_pairs={{28,0},{0,4},{4,8},{8,12},{12,16},{16,20},{20,24},{24,28},{29,1},{... | collective-permute-start | bytes 786440 | tf_op jit(solution)/shard_map/while/body/eval_jaxpr/ppermute | solution.py:10
  119.5 9.0 %collective-permute-start = (f32[256,256]{1,0:T(8,128)S(1)}, f32[256,256]{1,0:T(8,128)S(1)}, u32[]{:S(2)}, u32[]{:S(2)}) collective-permute-start(f32[256,256]{1,0:T(8,128)S(1)} %bitcast_add_fusion.2), channel_id=1, source_target_pairs={{28,0},{0,4},{4,8},{8,12},{12,16},{16,20},{20,24},{24,28},{29,1},{... | collective-permute-start | bytes 786440 | tf_op jit(solution)/shard_map/while/body/eval_jaxpr/ppermute | solution.py:10
  129.4 7.9 %collective-permute-start = (f32[256,256]{1,0:T(8,128)S(1)}, f32[256,256]{1,0:T(8,128)S(1)}, u32[]{:S(2)}, u32[]{:S(2)}) collective-permute-start(f32[256,256]{1,0:T(8,128)S(1)} %bitcast_add_fusion.2), channel_id=1, source_target_pairs={{28,0},{0,4},{4,8},{8,12},{12,16},{16,20},{20,24},{24,28},{29,1},{... | collective-permute-start | bytes 786440 | tf_op jit(solution)/shard_map/while/body/eval_jaxpr/ppermute | solution.py:10
  138.2 7.9 %collective-permute-start = (f32[256,256]{1,0:T(8,128)S(1)}, f32[256,256]{1,0:T(8,128)S(1)}, u32[]{:S(2)}, u32[]{:S(2)}) collective-permute-start(f32[256,256]{1,0:T(8,128)S(1)} %bitcast_add_fusion.2), channel_id=1, source_target_pairs={{28,0},{0,4},{4,8},{8,12},{12,16},{16,20},{20,24},{24,28},{29,1},{... | collective-permute-start | bytes 786440 | tf_op jit(solution)/shard_map/while/body/eval_jaxpr/ppermute | solution.py:10
  147.0 8.4 %collective-permute-start = (f32[256,256]{1,0:T(8,128)S(1)}, f32[256,256]{1,0:T(8,128)S(1)}, u32[]{:S(2)}, u32[]{:S(2)}) collective-permute-start(f32[256,256]{1,0:T(8,128)S(1)} %bitcast_add_fusion.2), channel_id=1, source_target_pairs={{28,0},{0,4},{4,8},{8,12},{12,16},{16,20},{20,24},{24,28},{29,1},{... | collective-permute-start | bytes 786440 | tf_op jit(solution)/shard_map/while/body/eval_jaxpr/ppermute | solution.py:10
  156.3 9.2 %collective-permute-start = (f32[256,256]{1,0:T(8,128)S(1)}, f32[256,256]{1,0:T(8,128)S(1)}, u32[]{:S(2)}, u32[]{:S(2)}) collective-permute-start(f32[256,256]{1,0:T(8,128)S(1)} %bitcast_add_fusion.2), channel_id=1, source_target_pairs={{28,0},{0,4},{4,8},{8,12},{12,16},{16,20},{20,24},{24,28},{29,1},{... | collective-permute-start | bytes 786440 | tf_op jit(solution)/shard_map/while/body/eval_jaxpr/ppermute | solution.py:10
  166.4 9.5 %collective-permute-start = (f32[256,256]{1,0:T(8,128)S(1)}, f32[256,256]{1,0:T(8,128)S(1)}, u32[]{:S(2)}, u32[]{:S(2)}) collective-permute-start(f32[256,256]{1,0:T(8,128)S(1)} %bitcast_add_fusion.2), channel_id=1, source_target_pairs={{28,0},{0,4},{4,8},{8,12},{12,16},{16,20},{20,24},{24,28},{29,1},{... | collective-permute-start | bytes 786440 | tf_op jit(solution)/shard_map/while/body/eval_jaxpr/ppermute | solution.py:10
  176.8 9.2 %collective-permute-start = (f32[256,256]{1,0:T(8,128)S(1)}, f32[256,256]{1,0:T(8,128)S(1)}, u32[]{:S(2)}, u32[]{:S(2)}) collective-permute-start(f32[256,256]{1,0:T(8,128)S(1)} %bitcast_add_fusion.2), channel_id=1, source_target_pairs={{28,0},{0,4},{4,8},{8,12},{12,16},{16,20},{20,24},{24,28},{29,1},{... | collective-permute-start | bytes 786440 | tf_op jit(solution)/shard_map/while/body/eval_jaxpr/ppermute | solution.py:10
Sparse Core Ops, SparseCore 0:
  10.1 40.2 all-gather.1
  68.9 23.7 reduce-scatter.1
  98.7 131.8 all-reduce.1
where the time goes:
time: 243 us
  waiting for transfers between devices  134 us (55%)
  blocking collectives  54.5 us (22%)
  matrix products  16.7 us (7%)
  local copies, waits for them, and re-layouts  16.3 us (7%)
  between operations  14.6 us (6%)
  other arithmetic  4.1 us (2%)
  starting transfers between devices  2.45 us (1%)
    ppermute x8, waiting for transfers between devices, shifted(): return lax.ppermute(block, axis, route)  68.5 us
    psum x1, blocking collectives, per_device(): lax.psum((local_weight, local_bias), ('blk', 'rep'))  47.3 us
    all_gather x1, waiting for transfers between devices, per_device(): piece = lax.all_gather(features, 'blk', axis=0, tiled=True)  40.9 us
    reduce_scatter x1, waiting for transfers between devices, per_device(): lax.psum_scatter(summed.reshape(rep_count * own_rows, feat_width), 'rep',...  23.8 us
    gather x1, local copies, waits for them, and re-layouts, per_device(): jnp.take(piece, clipped.reshape(-1), axis=0)  9.83 us
    all_gather x1, blocking collectives, per_device(): lax.all_gather(agg_grad, 'rep', axis=0, tiled=True)  7.17 us
    dot_general x8, matrix products, column_terms(): jnp.einsum('sp,sjf->pjf', col_onehot, contribution, precision=highest)  6.58 us
  transfers between devices with their start and end apart: 11, of which 10 were waited for; matrix products, arithmetic and copies ran while one was open for 6% of the time, Pallas kernels for 0%

commit v1 on v0

--- a/solution.py
+++ b/solution.py
@@ -48,7 +48,7 @@
     ).astype(jnp.bfloat16)
     local_weight = jnp.dot(aggregate.T, act_grad, preferred_element_type=jnp.float32)
     local_bias = jnp.sum(act_grad.astype(jnp.float32), axis=0)
-    weight_grad, bias_grad = lax.psum((local_weight, local_bias), ("blk", "rep"))
+    weight_grad, bias_grad = lax.psum(lax.psum((local_weight, local_bias), "blk"), "rep")
     scale_factor = 1.0 / (blk_count * rep_count)
     weight_grad = weight_grad * scale_factor
     bias_grad = bias_grad * scale_factor

time: 243 us -> 259 us (1.066)
  waiting for transfers between devices: 134 us -> 168 us
  blocking collectives: 54.5 us -> 34.7 us
    psum x1 -> x2, waiting for transfers between devices: 0.01 us -> 32.2 us  [the longest x1 32.2 us: per_device(): lax.psum(lax.psum((local_weight, local_bias), 'blk'), 'rep')]
    psum x1 -> x2, blocking collectives: 47.3 us -> 27.5 us  [the longest x1 21.9 us: per_device(): lax.psum((local_weight, local_bias), 'blk')]
  transfers between devices with their start and end apart: 11 -> 12, of which waited for: 10 -> 11; matrix products, arithmetic and copies ran while one was open for 6% -> 5% of each run, Pallas kernels for 0% -> 0%
where the time goes in v1:
time: 259 us; the launch traced here: 256 us
  waiting for transfers between devices  168 us (65%)
  blocking collectives  34.7 us (13%)
  matrix products  16.7 us (6%)
  local copies, waits for them, and re-layouts  16.2 us (6%)
  between operations  14.6 us (6%)
  other arithmetic  4.1 us (2%)
    ppermute x8, waiting for transfers between devices, shifted(): return lax.ppermute(block, axis, route)  70 us
    all_gather x1, waiting for transfers between devices, per_device(): piece = lax.all_gather(features, 'blk', axis=0, tiled=True)  40.9 us
    psum x1, waiting for transfers between devices, per_device(): lax.psum(lax.psum((local_weight, local_bias), 'blk'), 'rep')  32.2 us
    reduce_scatter x1, waiting for transfers between devices, per_device(): lax.psum_scatter(summed.reshape(rep_count * own_rows, feat_width), 'rep',...  23.8 us
    psum x1, blocking collectives, per_device(): lax.psum((local_weight, local_bias), 'blk')  21.9 us
    gather x1, local copies, waits for them, and re-layouts, per_device(): jnp.take(piece, clipped.reshape(-1), axis=0)  9.81 us
    all_gather x1, blocking collectives, per_device(): lax.all_gather(agg_grad, 'rep', axis=0, tiled=True)  7.16 us
    dot_general x8, matrix products, column_terms(): jnp.einsum('sp,sjf->pjf', col_onehot, contribution, precision=highest)  6.57 us
  transfers between devices with their start and end apart: 12, of which 11 were waited for; matrix products, arithmetic and copies ran while one was open for 5% of the time, Pallas kernels for 0%

profile of v1, /device:TPU:10, one launch (start us, length us, event | category | flops | bytes accessed | tf_op | source)
XLA Modules:
  0.0 256.3 jit_solution(17470063217702196965)
XLA Ops:
  7.2 0.7 all-gather.2.cloned.1.call-update
  8.6 0.7 multiply_bitcast_fusion.1
  9.3 0.1 fusion.25
  9.4 0.1 fusion.22
  9.5 40.9 %all-gather.2.cloned.1.call-done = bf16[2048,256]{1,0:T(8,128)(2,1)} async-done(((bf16[256,256]{1,0:T(8,128)(2,1)}), bf16[2048,256]{1,0:T(8,128)(2,1)}) %all-gather.2.cloned.1.call-update) | async-done | bytes 1048592 | tf_op jit(solution)/shard_map/all_gather | solution.py:27
  50.4 9.8 %gather_fusion = bf16[2048,256]{1,0:T(8,128)(2,1)} fusion(bf16[2048,256]{1,0:T(8,128)(2,1)} %all-gather.2.cloned.1.call-done, s32[2048]{0:T(1024)S(1)} %broadcast_clamp_fusion), kind=kCustom, calls=%fused_computation | custom fusion | bytes 2105344 | tf_op jit(solution)/shard_map/jit(_take)/gather | solution.py:31
  60.2 2.3 fusion.8
  62.6 2.1 copy.18
  64.6 2.7 %fusion.5 = f32[8,128,256]{2,0,1:T(8,128)S(1)} fusion(f32[16,256,128]{1,0,2:T(8,128)} %copy.18, f32[16]{0:T(128)S(1)} %compare_convert_fusion, s32[16]{0:T(128)S(1)} %bitcast.53), kind=kOutput, calls=%fused_computation.9 | convolution fusion | flops 50331904 | bytes 3145856 | tf_op jit(solution)/shard_map/st,sif->tif/dot_general | solution.py:39
  67.4 1.3 copy.15
  68.8 23.8 %reduce-scatter.2.cloned.1.call-done = f32[256,256]{1,0:T(8,128)} async-done(((f32[1024,256]{1,0:T(8,128)}), f32[256,256]{1,0:T(8,128)}) %reduce-scatter.2.cloned.1.call-update) | async-done | bytes 262160 | tf_op jit(solution)/shard_map/reduce_scatter | solution.py:40
  92.6 2.0 convert_reduce_fusion
  94.6 0.2 convolution_convert_fusion
  94.8 0.9 fusion.19
  95.8 7.2 %all_gather.7 = bf16[1024,256]{1,0:T(8,128)(2,1)S(1)} all-gather(bf16[256,256]{1,0:T(8,128)(2,1)S(1)} %convolution_convert_fusion), channel_id=1, replica_groups=mesh['blk'=8,'rep'=4] {'rep'}, dimensions={0}, use_global_device_ids=true | all-gather | bytes 655360 | tf_op jit(solution)/shard_map/all_gather | solution.py:56
  103.0 0.6 gather_fusion.1
  103.6 1.9 multiply_bitcast_fusion
  105.5 2.2 copy.17
  107.8 79.3 %while.15 = (s32[]{:T(128)}, f32[256,256]{1,0:T(8,128)S(1)}, s32[1,16]{1,0:T(1,128)S(1)}, s32[]{:T(128)}, f32[16,128,256]{2,0,1:T(8,128)S(1)}, /*index=5*/s32[]{...) while((s32[]{:T(128)}, f32[256,256]{1,0:T(8,128)S(1)}, ...), condition=%wide.region_2.3_spmd, body=%wide.region_1.2_spmd.sunk | while | flops 12648512 | bytes 4719116 | solution.py:78
  107.9 0.8 fusion.46
  108.8 1.5 collective-permute-start
  110.3 8.5 %collective-permute-done = f32[256,256]{1,0:T(8,128)S(1)} collective-permute-done((f32[256,256]{1,0:T(8,128)S(1)}, f32[256,256]{1,0:T(8,128)S(1)}, u32[]{:S(2)}, u32[]{:S(2)}) %collective-permute-start) | collective-permute-done | bytes 262176 | tf_op jit(solution)/shard_map/while/body/eval_jaxpr/ppermute | solution.py:10
  118.8 0.8 fusion.46
  119.7 0.1 collective-permute-start
  119.8 9.3 %collective-permute-done = f32[256,256]{1,0:T(8,128)S(1)} collective-permute-done((f32[256,256]{1,0:T(8,128)S(1)}, f32[256,256]{1,0:T(8,128)S(1)}, u32[]{:S(2)}, u32[]{:S(2)}) %collective-permute-start) | collective-permute-done | bytes 262176 | tf_op jit(solution)/shard_map/while/body/eval_jaxpr/ppermute | solution.py:10
  129.1 0.8 fusion.46
  130.0 0.1 collective-permute-start
  130.0 7.7 %collective-permute-done = f32[256,256]{1,0:T(8,128)S(1)} collective-permute-done((f32[256,256]{1,0:T(8,128)S(1)}, f32[256,256]{1,0:T(8,128)S(1)}, u32[]{:S(2)}, u32[]{:S(2)}) %collective-permute-start) | collective-permute-done | bytes 262176 | tf_op jit(solution)/shard_map/while/body/eval_jaxpr/ppermute | solution.py:10
  137.8 0.8 fusion.46
  138.7 0.1 collective-permute-start
  138.8 8.4 %collective-permute-done = f32[256,256]{1,0:T(8,128)S(1)} collective-permute-done((f32[256,256]{1,0:T(8,128)S(1)}, f32[256,256]{1,0:T(8,128)S(1)}, u32[]{:S(2)}, u32[]{:S(2)}) %collective-permute-start) | collective-permute-done | bytes 262176 | tf_op jit(solution)/shard_map/while/body/eval_jaxpr/ppermute | solution.py:10
  147.1 0.8 fusion.46
  148.0 0.1 collective-permute-start
  148.1 8.0 %collective-permute-done = f32[256,256]{1,0:T(8,128)S(1)} collective-permute-done((f32[256,256]{1,0:T(8,128)S(1)}, f32[256,256]{1,0:T(8,128)S(1)}, u32[]{:S(2)}, u32[]{:S(2)}) %collective-permute-start) | collective-permute-done | bytes 262176 | tf_op jit(solution)/shard_map/while/body/eval_jaxpr/ppermute | solution.py:10
  156.2 0.8 fusion.46
  157.1 0.1 collective-permute-start
  157.1 10.2 %collective-permute-done = f32[256,256]{1,0:T(8,128)S(1)} collective-permute-done((f32[256,256]{1,0:T(8,128)S(1)}, f32[256,256]{1,0:T(8,128)S(1)}, u32[]{:S(2)}, u32[]{:S(2)}) %collective-permute-start) | collective-permute-done | bytes 262176 | tf_op jit(solution)/shard_map/while/body/eval_jaxpr/ppermute | solution.py:10
  167.3 0.8 fusion.46
  168.2 0.1 collective-permute-start
  168.3 8.3 %collective-permute-done = f32[256,256]{1,0:T(8,128)S(1)} collective-permute-done((f32[256,256]{1,0:T(8,128)S(1)}, f32[256,256]{1,0:T(8,128)S(1)}, u32[]{:S(2)}, u32[]{:S(2)}) %collective-permute-start) | collective-permute-done | bytes 262176 | tf_op jit(solution)/shard_map/while/body/eval_jaxpr/ppermute | solution.py:10
  176.5 0.8 fusion.46
  177.5 9.6 %collective-permute-done = f32[256,256]{1,0:T(8,128)S(1)} collective-permute-done((f32[256,256]{1,0:T(8,128)S(1)}, f32[256,256]{1,0:T(8,128)S(1)}, u32[]{:S(2)}, u32[]{:S(2)}) %collective-permute-start) | collective-permute-done | bytes 262176 | tf_op jit(solution)/shard_map/while/body/eval_jaxpr/ppermute | solution.py:10
  187.1 0.7 convert_element_type.42
  187.8 21.9 %psum.30 = f32[256]{0:T(256)S(1)} all-reduce(f32[256]{0:T(256)S(1)} %get-tuple-element.160), channel_id=1, replica_groups=mesh['blk'=8,'rep'=4] {'blk'}, use_global_device_ids=true, to_apply=%region_6.7 | all-reduce | flops 256 | bytes 2048 | tf_op jit(solution)/shard_map/psum | solution.py:51
  209.7 5.7 %psum.31 = f32[256]{0:T(256)S(1)} all-reduce(f32[256]{0:T(256)S(1)} %psum.30), channel_id=1, replica_groups=mesh['blk'=8,'rep'=4] {'rep'}, use_global_device_ids=true, to_apply=%region_7.8 | all-reduce | flops 256 | bytes 2048 | tf_op jit(solution)/shard_map/psum | solution.py:51
  215.4 0.6 broadcast_multiply_fusion.1
  215.9 32.2 %all-reduce.5.cloned.1.call-done = f32[256,256]{1,0:T(8,128)} async-done(((f32[256,256]{1,0:T(8,128)}), f32[256,256]{1,0:T(8,128)}) %all-reduce.5.cloned.1.call-update) | async-done | bytes 262160 | tf_op jit(solution)/shard_map/psum | solution.py:51
  248.1 1.7 broadcast_multiply_fusion
  (54 shorter events, 0.9 us)
Async XLA Ops:
  7.2 53.1 %copy-start = (bf16[1,16,128,128]{3,2,1,0:T(8,128)(2,1)S(1)}, bf16[1,16,128,128]{3,2,1,0:T(8,128)(2,1)}, u32[]{:S(2)}) copy-start(bf16[1,16,128,128]{3,2,1,0:T(8,128)(2,1)} %param.11) | copy-start | bytes 1572868
  7.2 43.2 %all-gather.2.cloned.1.call-start = ((), (), s32[]{:S(2)}) async-start(), calls=%async_computation.1 | async-start | bytes 1179648 | tf_op jit(solution)/shard_map/all_gather | solution.py:27
  7.9 84.7 %reduce-scatter.2.cloned.1.call-start = ((), (), s32[]{:S(2)}) async-start(), calls=%async_computation.2 | async-start | bytes 1310720 | tf_op jit(solution)/shard_map/reduce_scatter | solution.py:40
  62.6 2.1 copy-start.4
  67.4 25.2 %copy-start.2 = (bf16[256,256]{1,0:T(8,128)(2,1)S(1)}, bf16[256,256]{1,0:T(8,128)(2,1)}, u32[]{:S(2)}) copy-start(bf16[256,256]{1,0:T(8,128)(2,1)} %param.15) | copy-start | bytes 393220
  67.4 25.2 %copy-start.5 = (bf16[256,256]{1,0:T(8,128)(2,1)S(1)}, bf16[256,256]{1,0:T(8,128)(2,1)}, u32[]{:S(2)}) copy-start(bf16[256,256]{1,0:T(8,128)(2,1)} %param.17) | copy-start | bytes 393220
  67.4 25.2 %copy-start.6 = (f32[256]{0:T(256)S(1)}, f32[256]{0:T(256)}, u32[]{:S(2)}) copy-start(f32[256]{0:T(256)} %param.16) | copy-start | bytes 3076
  68.7 146.6 %all-reduce.3.cloned.1.call-start = ((), (), s32[]{:S(2)}) async-start(), calls=%async_computation.3 | async-start | bytes 524288 | tf_op jit(solution)/shard_map/psum | solution.py:51
  92.6 2.2 copy-start.1
  95.8 152.4 %all-reduce.5.cloned.1.call-start = ((), (), s32[]{:S(2)}) async-start(), calls=%async_computation.4 | async-start | bytes 524288 | tf_op jit(solution)/shard_map/psum | solution.py:51
  105.5 2.3 copy-start.3
  108.8 10.0 %collective-permute-start = (f32[256,256]{1,0:T(8,128)S(1)}, f32[256,256]{1,0:T(8,128)S(1)}, u32[]{:S(2)}, u32[]{:S(2)}) collective-permute-start(f32[256,256]{1,0:T(8,128)S(1)} %bitcast_add_fusion.2), channel_id=1, source_target_pairs={{28,0},{0,4},{4,8},{8,12},{12,16},{16,20},{20,24},{24,28},{29,1},{... | collective-permute-start | bytes 786440 | tf_op jit(solution)/shard_map/while/body/eval_jaxpr/ppermute | solution.py:10
  119.7 9.4 %collective-permute-start = (f32[256,256]{1,0:T(8,128)S(1)}, f32[256,256]{1,0:T(8,128)S(1)}, u32[]{:S(2)}, u32[]{:S(2)}) collective-permute-start(f32[256,256]{1,0:T(8,128)S(1)} %bitcast_add_fusion.2), channel_id=1, source_target_pairs={{28,0},{0,4},{4,8},{8,12},{12,16},{16,20},{20,24},{24,28},{29,1},{... | collective-permute-start | bytes 786440 | tf_op jit(solution)/shard_map/while/body/eval_jaxpr/ppermute | solution.py:10
  130.0 7.8 %collective-permute-start = (f32[256,256]{1,0:T(8,128)S(1)}, f32[256,256]{1,0:T(8,128)S(1)}, u32[]{:S(2)}, u32[]{:S(2)}) collective-permute-start(f32[256,256]{1,0:T(8,128)S(1)} %bitcast_add_fusion.2), channel_id=1, source_target_pairs={{28,0},{0,4},{4,8},{8,12},{12,16},{16,20},{20,24},{24,28},{29,1},{... | collective-permute-start | bytes 786440 | tf_op jit(solution)/shard_map/while/body/eval_jaxpr/ppermute | solution.py:10
  138.7 8.4 %collective-permute-start = (f32[256,256]{1,0:T(8,128)S(1)}, f32[256,256]{1,0:T(8,128)S(1)}, u32[]{:S(2)}, u32[]{:S(2)}) collective-permute-start(f32[256,256]{1,0:T(8,128)S(1)} %bitcast_add_fusion.2), channel_id=1, source_target_pairs={{28,0},{0,4},{4,8},{8,12},{12,16},{16,20},{20,24},{24,28},{29,1},{... | collective-permute-start | bytes 786440 | tf_op jit(solution)/shard_map/while/body/eval_jaxpr/ppermute | solution.py:10
  148.0 8.1 %collective-permute-start = (f32[256,256]{1,0:T(8,128)S(1)}, f32[256,256]{1,0:T(8,128)S(1)}, u32[]{:S(2)}, u32[]{:S(2)}) collective-permute-start(f32[256,256]{1,0:T(8,128)S(1)} %bitcast_add_fusion.2), channel_id=1, source_target_pairs={{28,0},{0,4},{4,8},{8,12},{12,16},{16,20},{20,24},{24,28},{29,1},{... | collective-permute-start | bytes 786440 | tf_op jit(solution)/shard_map/while/body/eval_jaxpr/ppermute | solution.py:10
  157.1 10.3 %collective-permute-start = (f32[256,256]{1,0:T(8,128)S(1)}, f32[256,256]{1,0:T(8,128)S(1)}, u32[]{:S(2)}, u32[]{:S(2)}) collective-permute-start(f32[256,256]{1,0:T(8,128)S(1)} %bitcast_add_fusion.2), channel_id=1, source_target_pairs={{28,0},{0,4},{4,8},{8,12},{12,16},{16,20},{20,24},{24,28},{29,1},{... | collective-permute-start | bytes 786440 | tf_op jit(solution)/shard_map/while/body/eval_jaxpr/ppermute | solution.py:10
  168.2 8.3 %collective-permute-start = (f32[256,256]{1,0:T(8,128)S(1)}, f32[256,256]{1,0:T(8,128)S(1)}, u32[]{:S(2)}, u32[]{:S(2)}) collective-permute-start(f32[256,256]{1,0:T(8,128)S(1)} %bitcast_add_fusion.2), channel_id=1, source_target_pairs={{28,0},{0,4},{4,8},{8,12},{12,16},{16,20},{20,24},{24,28},{29,1},{... | collective-permute-start | bytes 786440 | tf_op jit(solution)/shard_map/while/body/eval_jaxpr/ppermute | solution.py:10
  177.4 9.7 %collective-permute-start = (f32[256,256]{1,0:T(8,128)S(1)}, f32[256,256]{1,0:T(8,128)S(1)}, u32[]{:S(2)}, u32[]{:S(2)}) collective-permute-start(f32[256,256]{1,0:T(8,128)S(1)} %bitcast_add_fusion.2), channel_id=1, source_target_pairs={{28,0},{0,4},{4,8},{8,12},{12,16},{16,20},{20,24},{24,28},{29,1},{... | collective-permute-start | bytes 786440 | tf_op jit(solution)/shard_map/while/body/eval_jaxpr/ppermute | solution.py:10
Sparse Core Ops, SparseCore 0:
  10.1 40.2 all-gather.1
  68.8 23.7 reduce-scatter.1
  96.5 75.0 all-reduce.2
  215.5 32.6 all-reduce.4
